TPU v7x, 32 devices: a whole 2x2x4 slice. The times are simulated.
32 devices in a mesh: row: 8 (over z, core), col: 4 (over y, x).
Axes of the slice: x: 2, y: 2, z: 4, core: 2. Of those that a mesh axis runs over, the one named last changes fastest.
Arguments:
- tiles: bfloat16 [4096, 128, 128], P(('row', 'col')), may hold values from -48 to 48
- tile_rows: int32 [4096], P(('row', 'col')), may hold values from 0 to 1023, as said below
- tile_cols: int32 [4096], P(('row', 'col')), may hold values from 0 to 1023, as said below
- tile_count: int32 [32], P(('row', 'col')), may hold values from 32 to 128, as said below
- degree: int32 [1024, 128], P(('row', 'col')), may hold values from 32 to 96
- labels: int32 [1024, 128], P(('row', 'col')), may hold values from 0 to 63
Outputs:
- scores: float32 [1024, 16, 128], P(('row', 'col'))
Inputs may be any that keep to these rules, and one draw needn't show every extreme that they name: tile_rows of the slots of device (r, c) lie in node-row blocks r * 128 to (r + 1) * 128 - 1. tile_cols of the slots of device (r, c) lie in node blocks (s * 4 + c) * 32 + o for some s below 8 and o below 32. `tile_count`: some device has all its slots live.
All inputs are finite; a program needn't handle non-finite values.
Results may differ from a plain program's by a relative error of at most 0.0039.
Values may be sent and summed in bfloat16 or wider, within the bound.
No kernel may reach another device: no remote copies, remote signals or barrier semaphores. Data moves between devices by JAX's collectives and lax.ppermute only.
A program may use at most 64 MiB of HBM per device.

v0:
```python
import jax
import jax.numpy as jnp
from jax import lax
from jax.sharding import PartitionSpec as P

QC = 16
ITERS = 2


def local(tiles, tile_rows, tile_cols, tile_count, degree, labels):
    ncol = lax.axis_size("col")
    row_pos = lax.axis_index("row")
    blk_dev = labels.shape[0]
    rblk = blk_dev * ncol
    scale = 1.0 / jnp.sqrt(degree.astype(jnp.float32))
    qidx = jnp.arange(QC, dtype=jnp.int32)
    prior = (labels[:, None, :] == qidx[None, :, None]).astype(jnp.float32)
    local_rows = tile_rows - row_pos * rblk
    owner = tile_cols // blk_dev
    local_cols = owner // ncol * blk_dev + tile_cols % blk_dev
    live = (jnp.arange(tiles.shape[0], dtype=jnp.int32) < tile_count[0]).astype(jnp.float32)
    field = prior
    for step in range(ITERS):
        if step == 0:
            own = (field * scale[:, None, :]).astype(jnp.bfloat16)
            gathered = lax.all_gather(own, "row", axis=0, tiled=True)
        else:
            own = (field * scale[:, None, :]).astype(jnp.bfloat16)
            gathered = lax.all_gather(own, "row", axis=0, tiled=True)
        picked = gathered[local_cols]
        terms = jnp.einsum("tqj,tij->tqi", picked, tiles, preferred_element_type=jnp.float32)
        terms = terms * live[:, None, None]
        partial_rows = jax.ops.segment_sum(terms, local_rows, num_segments=rblk)
        summed = lax.psum_scatter(partial_rows, "col", scatter_dimension=0, tiled=True)
        field = 0.8 * scale[:, None, :] * summed + 0.2 * prior
    return field


def solution(mesh):
    return jax.shard_map(
        local,
        mesh=mesh,
        in_specs=(
            P(("row", "col"), None, None),
            P(("row", "col")),
            P(("row", "col")),
            P(("row", "col")),
            P(("row", "col"), None),
            P(("row", "col"), None),
        ),
        out_specs=P(("row", "col"), None, None),
        check_vma=False,
    )
```

profile of v0, /device:TPU:0, one launch (start us, length us, event | category | flops | bytes accessed | tf_op | source)
XLA Modules:
  0.0 146.3 jit_solution(1190749417528610300)
XLA Ops:
  6.5 0.0 all-gather.3.cloned.1.call-start
  6.5 0.7 broadcast_multiply_fusion
  7.3 1.4 select_convert_fusion
  8.7 0.0 all-gather.3.cloned.1.call-update
  8.7 0.0 reduce-scatter.3.cloned.1.call-start
  9.4 0.7 compare_select_fusion
  10.1 0.7 broadcast_subtract_fusion
  10.8 23.0 %all-gather.3.cloned.1.call-done = bf16[256,16,128]{2,1,0:T(8,128)(2,1)} async-done(((bf16[32,16,128]{2,1,0:T(8,128)(2,1)}), bf16[256,16,128]{2,1,0:T(8,128)(2,1)}) %all-gather.3.cloned.1.call-update) | async-done | bytes 1048592 | tf_op jit(solution)/shard_map/all_gather | solution.py:26
  33.8 1.9 %gather_fusion = bf16[128,16,128]{2,1,0:T(8,128)(2,1)S(1)} fusion(bf16[256,16,128]{2,1,0:T(8,128)(2,1)} %all-gather.3.cloned.1.call-done, s32[1024]{0:T(1024)S(1)} %pad_clamp_fusion), kind=kCustom, calls=%fused_computation | custom fusion | bytes 1049088 | tf_op jit(solution)/shard_map/gather | solution.py:30
  35.7 0.0 copy-start.2
  35.7 4.5 %convolution_multiply_fusion.1 = f32[128,16,128]{2,1,0:T(8,128)S(1)} fusion(bf16[128,16,128]{2,1,0:T(8,128)(2,1)S(1)} %gather_fusion, bf16[128,128,128]{2,1,0:T(8,128)(2,1)} %param.6, f32[128]{0:T(128)S(1)} %compare_convert_fusion), kind=kOutput, calls=%fused_computation.5 | convolution fusion | flops 67371008 | bytes 5767680 | tf_op jit(solution)/shard_map/tqj,tij->tqi/dot_general | solution.py:31
  40.2 0.1 broadcast.42.clone
  40.3 5.2 %scatter_fusion = f32[128,16,128]{2,1,0:T(8,128)S(1)} fusion(f32[128,16,128]{2,1,0:T(8,128)S(1)} %broadcast.42.clone, s32[128]{0:T(128)S(1)} %broadcast_subtract_fusion, f32[128,16,128]{2,1,0:T(8,128)S(1)} %convolution_multiply_fusion.1), kind=kCustom, calls=%fused_computation.2 | custom fusion | flops 262144 | bytes 3146240 | tf_op jit(solution)/shard_map/scatter-add | solution.py:33
  45.5 0.0 copy-start.1
  45.5 1.0 copy-done.1
  46.4 0.0 reduce-scatter.3.cloned.1.call-update
  46.5 0.0 all-gather.5.cloned.1.call-start
  46.5 27.5 %reduce-scatter.3.cloned.1.call-done = f32[32,16,128]{2,1,0:T(8,128)} async-done(((f32[128,16,128]{2,1,0:T(8,128)}), f32[32,16,128]{2,1,0:T(8,128)}) %reduce-scatter.3.cloned.1.call-update) | async-done | bytes 262160 | tf_op jit(solution)/shard_map/reduce_scatter | solution.py:34
  74.0 0.0 copy-done.2
  74.0 1.7 %fusion.1 = bf16[32,16,128]{2,1,0:T(8,128)(2,1)} fusion(f32[32,16,128]{2,1,0:T(8,128)} %reduce-scatter.3.cloned.1.call-done, f32[32,128]{1,0:T(8,128)S(1)} %get-tuple-element.6, s32[32,128]{1,0:T(8,128)S(1)} %copy-done.2, f32[32,128]{1,0:T(8,128)S(1)} %get-tuple-element.5), kind=kLoop, calls=%fused_computation.9 | loop fusion | flops 393216 | bytes 442368 | tf_op jit(solution)/shard_map/convert_element_type | solution.py:28
  75.7 0.0 all-gather.5.cloned.1.call-update
  75.7 0.0 reduce-scatter.5.cloned.1.call-start
  75.7 22.2 %all-gather.5.cloned.1.call-done = bf16[256,16,128]{2,1,0:T(8,128)(2,1)} async-done(((bf16[32,16,128]{2,1,0:T(8,128)(2,1)}), bf16[256,16,128]{2,1,0:T(8,128)(2,1)}) %all-gather.5.cloned.1.call-update) | async-done | bytes 1048592 | tf_op jit(solution)/shard_map/all_gather | solution.py:29
  97.9 1.9 %gather_fusion.1 = bf16[128,16,128]{2,1,0:T(8,128)(2,1)S(1)} fusion(bf16[256,16,128]{2,1,0:T(8,128)(2,1)} %all-gather.5.cloned.1.call-done, s32[1024]{0:T(1024)S(1)} %pad_clamp_fusion), kind=kCustom, calls=%fused_computation.1 | custom fusion | bytes 1049088 | tf_op jit(solution)/shard_map/gather | solution.py:30
  99.9 4.5 %convolution_multiply_fusion = f32[128,16,128]{2,1,0:T(8,128)S(1)} fusion(bf16[128,16,128]{2,1,0:T(8,128)(2,1)S(1)} %gather_fusion.1, bf16[128,128,128]{2,1,0:T(8,128)(2,1)} %param.6, f32[128]{0:T(128)S(1)} %compare_convert_fusion), kind=kOutput, calls=%fused_computation.4 | convolution fusion | flops 67371008 | bytes 5767680 | tf_op jit(solution)/shard_map/tqj,tij->tqi/dot_general | solution.py:31
  104.3 0.1 broadcast.42
  104.4 5.2 %scatter_fusion.1 = f32[128,16,128]{2,1,0:T(8,128)S(1)} fusion(f32[128,16,128]{2,1,0:T(8,128)S(1)} %broadcast.42, s32[128]{0:T(128)S(1)} %broadcast_subtract_fusion, f32[128,16,128]{2,1,0:T(8,128)S(1)} %convolution_multiply_fusion), kind=kCustom, calls=%fused_computation.3 | custom fusion | flops 262144 | bytes 3146240 | tf_op jit(solution)/shard_map/scatter-add | solution.py:33
  109.6 0.0 copy-start
  109.6 1.0 copy-done
  110.6 0.0 reduce-scatter.5.cloned.1.call-update
  110.6 27.5 %reduce-scatter.5.cloned.1.call-done = f32[32,16,128]{2,1,0:T(8,128)} async-done(((f32[128,16,128]{2,1,0:T(8,128)}), f32[32,16,128]{2,1,0:T(8,128)}) %reduce-scatter.5.cloned.1.call-update) | async-done | bytes 262160 | tf_op jit(solution)/shard_map/reduce_scatter | solution.py:34
  138.1 1.7 %select_add_fusion = f32[32,16,128]{2,1,0:T(8,128)} fusion(f32[32,16,128]{2,1,0:T(8,128)} %reduce-scatter.5.cloned.1.call-done, s32[32,128]{1,0:T(8,128)S(1)} %copy-done.2, f32[32,128]{1,0:T(8,128)S(1)} %get-tuple-element.5), kind=kLoop, calls=%fused_computation.6 | loop fusion | flops 262144 | bytes 557056 | tf_op jit(solution)/shard_map/add | solution.py:35
  (2 shorter events, 0.0 us)
Async XLA Ops:
  6.5 27.3 %all-gather.3.cloned.1.call-start = ((), (), s32[]{:S(2)}) async-start(), calls=%async_computation.2 | async-start | bytes 1179648 | tf_op jit(solution)/shard_map/all_gather | solution.py:26
  8.7 65.3 %reduce-scatter.3.cloned.1.call-start = ((), (), s32[]{:S(2)}) async-start(), calls=%async_computation.3 | async-start | bytes 1310720 | tf_op jit(solution)/shard_map/reduce_scatter | solution.py:34
  35.7 38.3 %copy-start.2 = (s32[32,128]{1,0:T(8,128)S(1)}, s32[32,128]{1,0:T(8,128)}, u32[]{:S(2)}) copy-start(s32[32,128]{1,0:T(8,128)} %param.11) | copy-start | bytes 49156
  45.5 1.0 copy-start.1
  46.5 51.5 %all-gather.5.cloned.1.call-start = ((), (), s32[]{:S(2)}) async-start(), calls=%async_computation.4 | async-start | bytes 1179648 | tf_op jit(solution)/shard_map/all_gather | solution.py:29
  75.7 62.4 %reduce-scatter.5.cloned.1.call-start = ((), (), s32[]{:S(2)}) async-start(), calls=%async_computation.5 | async-start | bytes 1310720 | tf_op jit(solution)/shard_map/reduce_scatter | solution.py:34
  109.6 1.0 copy-start
Sparse Core Ops, SparseCore 0:
  9.0 24.7 all-gather.2
  46.6 27.3 reduce-scatter.2
  75.8 22.0 all-gather.4
  110.7 27.3 reduce-scatter.4
where the time goes:
time: 147 us; the launch traced here: 146 us
  waiting for transfers between devices  100 us (68%)
  other arithmetic  17.2 us (12%)
  between operations  13.9 us (9%)
  matrix products  8.93 us (6%)
  local copies, waits for them, and re-layouts  5.95 us (4%)
    reduce_scatter x2, waiting for transfers between devices, local(): lax.psum_scatter(partial_rows, 'col', scatter_dimension=0, tiled=True)  55 us
    all_gather x2, waiting for transfers between devices, local(): gathered = lax.all_gather(own, 'row', axis=0, tiled=True)  45.2 us
    scatter-add x2, other arithmetic, local(): partial_rows = jax.ops.segment_sum(terms, local_rows, num_segments=rblk)  10.3 us
    dot_general x2, matrix products, local(): jnp.einsum('tqj,tij->tqi', picked, tiles, preferred_element_type=jnp.floa...  8.93 us
    gather x2, local copies, waits for them, and re-layouts, local(): picked = gathered[local_cols]  3.85 us
    convert_element_type x2, other arithmetic, local(): own = (field * scale[:, None, :]).astype(jnp.bfloat16)  3.08 us
  transfers between devices with their start and end apart: 4, of which 4 were waited for; matrix products, arithmetic and copies ran while one was open for 1% of the time, Pallas kernels for 0%

commit v1 on v0

--- a/solution.py
+++ b/solution.py
@@ -5,6 +5,18 @@
 
 QC = 16
 ITERS = 2
+
+
+def doubled_up(x, axis, dim):
+    ways, here = (lax.axis_size(axis), lax.axis_index(axis))
+    grown, reach = (x, 1)
+    while reach < ways:
+        theirs = lax.ppermute(grown, axis, [(d, d ^ reach) for d in range(ways)])
+        mine_first = jnp.concatenate([grown, theirs], axis=dim)
+        theirs_first = jnp.concatenate([theirs, grown], axis=dim)
+        grown = jnp.where(here & reach == 0, mine_first, theirs_first)
+        reach = 2 * reach
+    return grown
 
 
 def local(tiles, tile_rows, tile_cols, tile_count, degree, labels):
@@ -26,7 +38,7 @@
             gathered = lax.all_gather(own, "row", axis=0, tiled=True)
         else:
             own = (field * scale[:, None, :]).astype(jnp.bfloat16)
-            gathered = lax.all_gather(own, "row", axis=0, tiled=True)
+            gathered = doubled_up(own, "row", 0)
         picked = gathered[local_cols]
         terms = jnp.einsum("tqj,tij->tqi", picked, tiles, preferred_element_type=jnp.float32)
         terms = terms * live[:, None, None]

time: 147 us -> 158 us (1.075)
  waiting for transfers between devices: 100 us -> 109 us
  starting transfers between devices: 0.13 us -> 4.19 us
    ppermute x0 -> x3, waiting for transfers between devices: none -> 31.1 us  [doubled_up(): theirs = lax.ppermute(grown, axis, [(d, d ^ reach) for d in range(ways)])]
    all_gather x2 -> x1, waiting for transfers between devices: 45.2 us -> 23 us  [local(): gathered = lax.all_gather(own, 'row', axis=0, tiled=True)]
    ppermute x0 -> x3, starting transfers between devices: none -> 4.1 us  [doubled_up(): theirs = lax.ppermute(grown, axis, [(d, d ^ reach) for d in range(ways)])]
  transfers between devices with their start and end apart: 4 -> 6, of which waited for: 4 -> 6; matrix products, arithmetic and copies ran while one was open for 1% -> 1% of each run, Pallas kernels for 0% -> 0%
where the time goes in v1:
time: 158 us
  waiting for transfers between devices  109 us (69%)
  other arithmetic  16.8 us (11%)
  between operations  13.9 us (9%)
  matrix products  8.93 us (6%)
  local copies, waits for them, and re-layouts  4.73 us (3%)
  starting transfers between devices  4.19 us (3%)
    reduce_scatter x2, waiting for transfers between devices, local(): lax.psum_scatter(partial_rows, 'col', scatter_dimension=0, tiled=True)  55.3 us
    ppermute x3, waiting for transfers between devices, doubled_up(): theirs = lax.ppermute(grown, axis, [(d, d ^ reach) for d in range(ways)])  31.1 us
    all_gather x1, waiting for transfers between devices, local(): gathered = lax.all_gather(own, 'row', axis=0, tiled=True)  23 us
    scatter-add x2, other arithmetic, local(): partial_rows = jax.ops.segment_sum(terms, local_rows, num_segments=rblk)  10.3 us
    dot_general x2, matrix products, local(): jnp.einsum('tqj,tij->tqi', picked, tiles, preferred_element_type=jnp.floa...  8.93 us
    ppermute x3, starting transfers between devices, doubled_up(): theirs = lax.ppermute(grown, axis, [(d, d ^ reach) for d in range(ways)])  4.1 us
  transfers between devices with their start and end apart: 6, of which 6 were waited for; matrix products, arithmetic and copies ran while one was open for 1% of the time, Pallas kernels for 0%

profile of v1, /device:TPU:0, one launch (start us, length us, event | category | flops | bytes accessed | tf_op | source)
XLA Modules:
  0.0 158.0 jit_solution(11974360401670630338)
XLA Ops:
  6.5 0.0 all-gather.2.cloned.1.call-start
  6.5 0.7 broadcast_multiply_fusion
  7.3 1.4 select_convert_fusion
  8.7 0.0 all-gather.2.cloned.1.call-update
  8.7 0.0 reduce-scatter.3.cloned.1.call-start
  9.4 0.7 compare_select_fusion
  10.1 0.7 broadcast_subtract_fusion
  10.8 23.0 %all-gather.2.cloned.1.call-done = bf16[256,16,128]{2,1,0:T(8,128)(2,1)} async-done(((bf16[32,16,128]{2,1,0:T(8,128)(2,1)}), bf16[256,16,128]{2,1,0:T(8,128)(2,1)}) %all-gather.2.cloned.1.call-update) | async-done | bytes 1048592 | tf_op jit(solution)/shard_map/all_gather | solution.py:38
  33.8 1.9 %gather_fusion = bf16[128,16,128]{2,1,0:T(8,128)(2,1)S(1)} fusion(bf16[256,16,128]{2,1,0:T(8,128)(2,1)} %all-gather.2.cloned.1.call-done, s32[1024]{0:T(1024)S(1)} %pad_clamp_fusion), kind=kCustom, calls=%fused_computation | custom fusion | bytes 1049088 | tf_op jit(solution)/shard_map/gather | solution.py:42
  35.7 0.0 copy-start.2
  35.7 4.5 %convolution_multiply_fusion.1 = f32[128,16,128]{2,1,0:T(8,128)S(1)} fusion(bf16[128,16,128]{2,1,0:T(8,128)(2,1)S(1)} %gather_fusion, bf16[128,128,128]{2,1,0:T(8,128)(2,1)} %param.6, f32[128]{0:T(128)S(1)} %compare_convert_fusion), kind=kOutput, calls=%fused_computation.5 | convolution fusion | flops 67371008 | bytes 5767680 | tf_op jit(solution)/shard_map/tqj,tij->tqi/dot_general | solution.py:43
  40.2 0.1 broadcast.44.clone
  40.3 5.2 %scatter_fusion = f32[128,16,128]{2,1,0:T(8,128)S(1)} fusion(f32[128,16,128]{2,1,0:T(8,128)S(1)} %broadcast.44.clone, s32[128]{0:T(128)S(1)} %broadcast_subtract_fusion, f32[128,16,128]{2,1,0:T(8,128)S(1)} %convolution_multiply_fusion.1), kind=kCustom, calls=%fused_computation.2 | custom fusion | flops 262144 | bytes 3146240 | tf_op jit(solution)/shard_map/scatter-add | solution.py:45
  45.5 0.0 copy-start.1
  45.5 1.0 copy-done.1
  46.4 0.0 reduce-scatter.3.cloned.1.call-update
  46.5 0.0 reduce-scatter.5.cloned.1.call-start
  46.5 27.5 %reduce-scatter.3.cloned.1.call-done = f32[32,16,128]{2,1,0:T(8,128)} async-done(((f32[128,16,128]{2,1,0:T(8,128)}), f32[32,16,128]{2,1,0:T(8,128)}) %reduce-scatter.3.cloned.1.call-update) | async-done | bytes 262160 | tf_op jit(solution)/shard_map/reduce_scatter | solution.py:46
  74.0 0.0 copy-done.2
  74.0 1.0 fusion.1
  75.0 0.1 collective-permute-start
  75.1 1.3 collective-permute-done
  76.4 1.6 collective-permute-start.1
  78.0 6.9 %collective-permute-done.1 = bf16[64,16,128]{2,1,0:T(8,128)(2,1)S(1)} collective-permute-done((bf16[64,16,128]{2,1,0:T(8,128)(2,1)S(1)}, bf16[64,16,128]{2,1,0:T(8,128)(2,1)S(1)}, u32[]{:S(2)}, u32[]{:S(2)}) %collective-permute-start.1) | collective-permute-done | bytes 262176 | tf_op jit(solution)/shard_map/ppermute | solution.py:14
  84.9 0.1 maximum_select_fusion.1
  85.0 2.5 %collective-permute-start.2 = (bf16[128,16,128]{2,1,0:T(8,128)(2,1)S(1)}, bf16[128,16,128]{2,1,0:T(8,128)(2,1)S(1)}, u32[]{:S(2)}, u32[]{:S(2)}) collective-permute-start(bf16[128,16,128]{2,1,0:T(8,128)(2,1)S(1)} %maximum_select_fusion.1), channel_id=1, source_target_pairs={{0,16},{4,20},{8,24},{12,28},{16,0},{20,4},{24,8},{28,12},{1,17},{... | collective-permute-start | bytes 1572872 | tf_op jit(solution)/shard_map/ppermute | solution.py:14
  87.4 22.9 %collective-permute-done.2 = bf16[128,16,128]{2,1,0:T(8,128)(2,1)S(1)} collective-permute-done((bf16[128,16,128]{2,1,0:T(8,128)(2,1)S(1)}, bf16[128,16,128]{2,1,0:T(8,128)(2,1)S(1)}, u32[]{:S(2)}, u32[]{:S(2)}) %collective-permute-start.2) | collective-permute-done | bytes 524320 | tf_op jit(solution)/shard_map/ppermute | solution.py:14
  110.3 0.2 maximum_select_fusion
  110.5 0.7 gather_fusion.1
  111.2 4.5 %convolution_multiply_fusion = f32[128,16,128]{2,1,0:T(8,128)S(1)} fusion(bf16[128,16,128]{2,1,0:T(8,128)(2,1)S(1)} %gather_fusion.1, bf16[128,128,128]{2,1,0:T(8,128)(2,1)} %param.6, f32[128]{0:T(128)S(1)} %compare_convert_fusion), kind=kOutput, calls=%fused_computation.4 | convolution fusion | flops 67371008 | bytes 5767680 | tf_op jit(solution)/shard_map/tqj,tij->tqi/dot_general | solution.py:43
  115.6 0.1 broadcast.44
  115.7 5.2 %scatter_fusion.1 = f32[128,16,128]{2,1,0:T(8,128)S(1)} fusion(f32[128,16,128]{2,1,0:T(8,128)S(1)} %broadcast.44, s32[128]{0:T(128)S(1)} %broadcast_subtract_fusion, f32[128,16,128]{2,1,0:T(8,128)S(1)} %convolution_multiply_fusion), kind=kCustom, calls=%fused_computation.3 | custom fusion | flops 262144 | bytes 3146240 | tf_op jit(solution)/shard_map/scatter-add | solution.py:45
  120.9 0.0 copy-start
  120.9 1.0 copy-done
  121.9 0.0 reduce-scatter.5.cloned.1.call-update
  121.9 27.9 %reduce-scatter.5.cloned.1.call-done = f32[32,16,128]{2,1,0:T(8,128)} async-done(((f32[128,16,128]{2,1,0:T(8,128)}), f32[32,16,128]{2,1,0:T(8,128)}) %reduce-scatter.5.cloned.1.call-update) | async-done | bytes 262160 | tf_op jit(solution)/shard_map/reduce_scatter | solution.py:46
  149.8 1.7 %select_add_fusion = f32[32,16,128]{2,1,0:T(8,128)} fusion(f32[32,16,128]{2,1,0:T(8,128)} %reduce-scatter.5.cloned.1.call-done, s32[32,128]{1,0:T(8,128)S(1)} %copy-done.2, f32[32,128]{1,0:T(8,128)S(1)} %get-tuple-element.5), kind=kLoop, calls=%fused_computation.8 | loop fusion | flops 262144 | bytes 557056 | tf_op jit(solution)/shard_map/add | solution.py:47
  (3 shorter events, 0.0 us)
Async XLA Ops:
  6.5 27.3 %all-gather.2.cloned.1.call-start = ((), (), s32[]{:S(2)}) async-start(), calls=%async_computation.2 | async-start | bytes 1179648 | tf_op jit(solution)/shard_map/all_gather | solution.py:38
  8.7 65.3 %reduce-scatter.3.cloned.1.call-start = ((), (), s32[]{:S(2)}) async-start(), calls=%async_computation.3 | async-start | bytes 1310720 | tf_op jit(solution)/shard_map/reduce_scatter | solution.py:46
  35.7 38.3 %copy-start.2 = (s32[32,128]{1,0:T(8,128)S(1)}, s32[32,128]{1,0:T(8,128)}, u32[]{:S(2)}) copy-start(s32[32,128]{1,0:T(8,128)} %param.11) | copy-start | bytes 49156
  45.5 1.0 copy-start.1
  46.5 103.3 %reduce-scatter.5.cloned.1.call-start = ((), (), s32[]{:S(2)}) async-start(), calls=%async_computation.4 | async-start | bytes 1310720 | tf_op jit(solution)/shard_map/reduce_scatter | solution.py:46
  75.0 1.4 collective-permute-start
  76.4 8.4 %collective-permute-start.1 = (bf16[64,16,128]{2,1,0:T(8,128)(2,1)S(1)}, bf16[64,16,128]{2,1,0:T(8,128)(2,1)S(1)}, u32[]{:S(2)}, u32[]{:S(2)}) collective-permute-start(bf16[64,16,128]{2,1,0:T(8,128)(2,1)S(1)} %maximum_select_fusion.2), channel_id=1, source_target_pairs={{0,8},{4,12},{8,0},{12,4},{16,24},{20,28},{24,16},{28,20},{1,9},{5... | collective-permute-start | bytes 786440 | tf_op jit(solution)/shard_map/ppermute | solution.py:14
  85.0 25.3 %collective-permute-start.2 = (bf16[128,16,128]{2,1,0:T(8,128)(2,1)S(1)}, bf16[128,16,128]{2,1,0:T(8,128)(2,1)S(1)}, u32[]{:S(2)}, u32[]{:S(2)}) collective-permute-start(bf16[128,16,128]{2,1,0:T(8,128)(2,1)S(1)} %maximum_select_fusion.1), channel_id=1, source_target_pairs={{0,16},{4,20},{8,24},{12,28},{16,0},{20,4},{24,8},{28,12},{1,17},{... | collective-permute-start | bytes 1572872 | tf_op jit(solution)/shard_map/ppermute | solution.py:14
  120.9 1.0 copy-start
Sparse Core Ops, SparseCore 0:
  9.0 24.7 all-gather.1
  46.6 27.3 reduce-scatter.2
  122.0 27.6 reduce-scatter.4
